TPU v7x, 512 devices: a whole 4x4x16 slice. The times are simulated.
512 devices in a mesh: rows: 64 (over z, y), cols: 8 (over x, core).
Axes of the slice: x: 4, y: 4, z: 16, core: 2. Of those that a mesh axis runs over, the one named last changes fastest.
Arguments:
- lower_pivot: bfloat16 [4, 2048, 4, 2048], P(None, 'rows', None, 'cols'), may hold values from -0.0625 to 0.0625
- lower_rest: bfloat16 [98304, 4, 2048], P('rows', None, 'cols'), may hold values from -0.0625 to 0.0625
- diag_inverse: bfloat16 [4, 2048, 2048], P(None, 'cols', 'rows'), may hold values from -0.125 to 0.125
- rhs_pivot: bfloat16 [4, 2048, 512], P(None, 'rows', 'cols'), may hold values from -6 to 6
- rhs_rest: bfloat16 [512, 98304], P('cols', 'rows'), may hold values from -6 to 6
Outputs:
- solution: bfloat16 [4, 2048, 512], P(None, 'cols')
- remainder: bfloat16 [512, 98304], P('cols', 'rows')
All inputs are finite; a program needn't handle non-finite values.
Results may differ from a plain program's by a relative error of at most 0.017.
Values may be sent and summed in bfloat16 or wider, within the bound.
A program may use at most 64 MiB of HBM per device.

v0:
```python
import jax
import jax.numpy as jnp
from jax import lax
from jax.sharding import PartitionSpec as P


def per_device(lower_pivot, lower_rest, diag_inverse, rhs_pivot, rhs_rest):
    block_count = lower_pivot.shape[0]
    pivot_rows = lower_pivot.shape[1]
    share_width = lower_pivot.shape[3]
    sides_share = rhs_pivot.shape[2]
    sides_total = sides_share * lax.axis_size("cols")
    rest_rows = lower_rest.shape[0]
    col_offset = lax.axis_index("cols") * sides_share
    solved = []
    for step_index in range(block_count):
        partials = jnp.zeros((pivot_rows, sides_total), jnp.float32)
        partials = lax.dynamic_update_slice(
            partials, rhs_pivot[step_index].astype(jnp.float32), (jnp.int32(0), col_offset)
        )
        if step_index > 0:
            factor_part = lower_pivot[step_index, :, :step_index, :].reshape(
                pivot_rows, step_index * share_width
            )
            known_part = jnp.concatenate(solved, axis=0)
            partials = partials - jnp.dot(
                factor_part, known_part, preferred_element_type=jnp.float32
            )
        residual = lax.psum(partials.astype(jnp.bfloat16), "cols")
        product = jnp.dot(diag_inverse[step_index], residual, preferred_element_type=jnp.float32)
        solved_block = lax.psum(product, "rows").astype(jnp.bfloat16)
        solved.append(solved_block)
    solution = jnp.stack(solved)
    flat_solution = solution.reshape(block_count * share_width, sides_total)
    flat_lower = lower_rest.reshape(rest_rows, block_count * share_width)
    total_sum = lax.psum_scatter(
        lax.dot_general(
            flat_solution, flat_lower, (((0,), (1,)), ((), ())), preferred_element_type=jnp.float32
        ).astype(jnp.bfloat16),
        "cols",
        scatter_dimension=0,
        tiled=True,
    ).astype(jnp.float32)
    remainder = (rhs_rest.astype(jnp.float32) - total_sum).astype(jnp.bfloat16)
    return (solution, remainder)


def solution(mesh):
    placed = (
        P(None, "rows", None, "cols"),
        P("rows", None, "cols"),
        P(None, "cols", "rows"),
        P(None, "rows", "cols"),
        P("cols", "rows"),
    )
    return jax.shard_map(
        per_device,
        mesh=mesh,
        in_specs=placed,
        out_specs=(P(None, "cols", None), P("cols", "rows")),
        check_vma=False,
    )
```

profile of v0, /device:TPU:8, one launch (start us, length us, event | category | flops | bytes accessed | tf_op | source)
XLA Modules:
  0.0 1294.9 jit_solution(7046899199717933439)
XLA Ops:
  7.2 0.0 copy-start
  7.2 0.0 reduce-scatter.2.cloned.1.call-start
  7.2 1.6 slice.36
  8.8 1.5 slice.39
  10.3 0.9 slice.42
  11.2 1.4 bitcast_convert_fusion.3
  12.6 0.3 dynamic_update_slice.12
  12.9 25.7 %psum.56 = bf16[32,512]{1,0:T(8,128)(2,1)S(1)} all-reduce(bf16[32,512]{1,0:T(8,128)(2,1)S(1)} %convert_element_type.62), channel_id=1, replica_groups=mesh['rows'=64,'cols'=8] {'cols'}, use_global_device_ids=true, to_apply=%region_0.0 | all-reduce | flops 16384 | bytes 65536 | tf_op jit(solution)/shard_map/psum | solution.py:29
  38.6 1.8 convolution_bitcast_fusion.4
  40.3 284.2 %all-reduce.4 = bf16[256,512]{0,1:T(8,128)(2,1)S(1)} all-reduce(f32[256,512]{0,1:T(8,128)} %convolution_bitcast_fusion.4), channel_id=1, replica_groups=mesh['rows'=64,'cols'=8] {'rows'}, use_global_device_ids=true, to_apply=%region_1.0 | all-reduce | flops 131072 | bytes 786432 | tf_op jit(solution)/shard_map/psum | solution.py:31
  324.5 0.9 dynamic_update_slice.13
  325.4 1.6 fusion.7
  327.0 24.2 %psum.58 = bf16[32,512]{1,0:T(8,128)(2,1)S(1)} all-reduce(bf16[32,512]{1,0:T(8,128)(2,1)} %fusion.7), channel_id=1, replica_groups=mesh['rows'=64,'cols'=8] {'cols'}, use_global_device_ids=true, to_apply=%region_2.0 | all-reduce | flops 16384 | bytes 65536 | tf_op jit(solution)/shard_map/psum | solution.py:29
  351.1 1.8 convolution_bitcast_fusion.3
  352.9 280.2 %all-reduce.5 = bf16[256,512]{0,1:T(8,128)(2,1)} all-reduce(f32[256,512]{0,1:T(8,128)} %convolution_bitcast_fusion.3), channel_id=1, replica_groups=mesh['rows'=64,'cols'=8] {'rows'}, use_global_device_ids=true, to_apply=%region_3.0 | all-reduce | flops 131072 | bytes 786432 | tf_op jit(solution)/shard_map/psum | solution.py:31
  633.1 1.4 copy.13
  634.5 0.9 dynamic_update_slice.14
  635.4 1.8 fusion.9
  637.2 24.2 %psum.60 = bf16[32,512]{1,0:T(8,128)(2,1)S(1)} all-reduce(bf16[32,512]{1,0:T(8,128)(2,1)} %fusion.9), channel_id=1, replica_groups=mesh['rows'=64,'cols'=8] {'cols'}, use_global_device_ids=true, to_apply=%region_4.0 | all-reduce | flops 16384 | bytes 65536 | tf_op jit(solution)/shard_map/psum | solution.py:29
  661.4 1.8 convolution_bitcast_fusion.2
  663.1 277.9 %all-reduce.6 = bf16[256,512]{0,1:T(8,128)(2,1)} all-reduce(f32[256,512]{0,1:T(8,128)} %convolution_bitcast_fusion.2), channel_id=1, replica_groups=mesh['rows'=64,'cols'=8] {'rows'}, use_global_device_ids=true, to_apply=%region_5.0 | all-reduce | flops 131072 | bytes 786432 | tf_op jit(solution)/shard_map/psum | solution.py:31
  941.1 0.3 dynamic_update_slice.15
  941.4 1.4 fusion.8
  942.8 23.6 %psum.62 = bf16[32,512]{1,0:T(8,128)(2,1)S(1)} all-reduce(bf16[32,512]{1,0:T(8,128)(2,1)S(1)} %fusion.8), channel_id=1, replica_groups=mesh['rows'=64,'cols'=8] {'cols'}, use_global_device_ids=true, to_apply=%region_6.0 | all-reduce | flops 16384 | bytes 65536 | tf_op jit(solution)/shard_map/psum | solution.py:29
  966.4 1.8 convolution_bitcast_fusion.1
  968.2 279.9 %all-reduce.7 = bf16[256,512]{0,1:T(8,128)(2,1)} all-reduce(f32[256,512]{0,1:T(8,128)} %convolution_bitcast_fusion.1), channel_id=1, replica_groups=mesh['rows'=64,'cols'=8] {'rows'}, use_global_device_ids=true, to_apply=%region_7.0 | all-reduce | flops 131072 | bytes 786432 | tf_op jit(solution)/shard_map/psum | solution.py:31
  1248.1 0.0 copy-done
  1248.1 4.1 fusion.1
  1252.2 0.0 reduce-scatter.2.cloned.1.call-update
  1252.2 2.2 pad_maximum_fusion
  1254.4 0.0 copy-start.1
  1254.4 2.3 copy.11
  1256.7 29.6 %reduce-scatter.2.cloned.1.call-done = bf16[64,1536]{1,0:T(8,128)(2,1)} async-done(((bf16[512,1536]{1,0:T(8,128)(2,1)}), bf16[64,1536]{1,0:T(8,128)(2,1)}) %reduce-scatter.2.cloned.1.call-update) | async-done | bytes 196624 | tf_op jit(solution)/shard_map/reduce_scatter | solution.py:36
  1286.4 0.0 copy-done.1
  1286.4 1.6 subtract_convert_fusion
  (6 shorter events, 0.0 us)
Async XLA Ops:
  7.2 1240.9 %copy-start = (bf16[1536,4,256]{2,1,0:T(4,128)(2,1)S(1)}, bf16[1536,4,256]{2,1,0:T(4,128)(2,1)}, u32[]{:S(2)}) copy-start(bf16[1536,4,256]{2,1,0:T(4,128)(2,1)} %param.6) | copy-start | bytes 9437188
  7.2 1279.2 %reduce-scatter.2.cloned.1.call-start = ((), (), s32[]{:S(2)}) async-start(), calls=%async_computation.1 | async-start | bytes 1769472 | tf_op jit(solution)/shard_map/reduce_scatter | solution.py:36
  1254.4 31.9 %copy-start.1 = (bf16[64,1536]{1,0:T(8,128)(2,1)S(1)}, bf16[64,1536]{1,0:T(8,128)(2,1)}, u32[]{:S(2)}) copy-start(bf16[64,1536]{1,0:T(8,128)(2,1)} %param.9) | copy-start | bytes 589828
Sparse Core Ops, SparseCore 0:
  1252.3 33.9 reduce-scatter.1
where the time goes:
time: 1300 us; the launch traced here: 1290 us
  blocking collectives  1220 us (94%)
  waiting for transfers between devices  29.6 us (2%)
  matrix products  15.9 us (1%)
  between operations  14.1 us (1%)
    psum x4, blocking collectives, per_device(): solved_block = lax.psum(product, 'rows').astype(jnp.bfloat16)  1120 us
    psum x4, blocking collectives, per_device(): residual = lax.psum(partials.astype(jnp.bfloat16), 'cols')  97.6 us
    reduce_scatter x1, waiting for transfers between devices, per_device(): lax.psum_scatter(lax.dot_general(flat_solution, flat_lower, (((0,), (1,))...  29.6 us
  transfers between devices with their start and end apart: 1, of which 1 were waited for; matrix products, arithmetic and copies ran while one was open for 0% of the time, Pallas kernels for 0%

commit v1 on v0

--- a/solution.py
+++ b/solution.py
@@ -26,7 +26,7 @@
             partials = partials - jnp.dot(
                 factor_part, known_part, preferred_element_type=jnp.float32
             )
-        residual = lax.psum(partials.astype(jnp.bfloat16), "cols")
+        residual = jnp.sum(lax.all_gather(partials.astype(jnp.bfloat16), "cols"), axis=0)
         product = jnp.dot(diag_inverse[step_index], residual, preferred_element_type=jnp.float32)
         solved_block = lax.psum(product, "rows").astype(jnp.bfloat16)
         solved.append(solved_block)

time: 1300 us -> 1260 us (0.969)
  blocking collectives: 1220 us -> 1180 us
    psum x4 -> x0, blocking collectives: 97.6 us -> none  [per_device(): residual = lax.psum(partials.astype(jnp.bfloat16), 'cols')]
    all_gather x0 -> x4, blocking collectives: none -> 54.9 us  [per_device(): lax.all_gather(partials.astype(jnp.bfloat16), 'cols')]
where the time goes in v1:
time: 1260 us
  blocking collectives  1180 us (94%)
  waiting for transfers between devices  31.3 us (2%)
  matrix products  14.7 us (1%)
  between operations  14.2 us (1%)
    psum x4, blocking collectives, per_device(): solved_block = lax.psum(product, 'rows').astype(jnp.bfloat16)  1120 us
    all_gather x4, blocking collectives, per_device(): lax.all_gather(partials.astype(jnp.bfloat16), 'cols')  54.9 us
    reduce_scatter x1, waiting for transfers between devices, per_device(): lax.psum_scatter(lax.dot_general(flat_solution, flat_lower, (((0,), (1,))...  31.3 us
  transfers between devices with their start and end apart: 1, of which 1 were waited for; matrix products, arithmetic and copies ran while one was open for 0% of the time, Pallas kernels for 0%

profile of v1, /device:TPU:8, one launch (start us, length us, event | category | flops | bytes accessed | tf_op | source)
XLA Modules:
  0.0 1255.1 jit_solution(11155757264880645641)
XLA Ops:
  7.2 0.0 copy-start
  7.2 0.0 reduce-scatter.2.cloned.1.call-start
  7.2 1.6 slice.36
  8.8 1.5 slice.39
  10.3 0.9 slice.42
  11.2 1.4 bitcast_convert_fusion.3
  12.6 0.3 dynamic_update_slice.12
  12.9 13.2 %all-gather = bf16[256,512]{1,0:T(8,128)(2,1)S(1)} all-gather(bf16[32,512]{1,0:T(8,128)(2,1)S(1)} %convert_element_type.70), channel_id=2, replica_groups=mesh['rows'=64,'cols'=8] {'cols'}, dimensions={0}, use_global_device_ids=true | all-gather | bytes 294912 | tf_op jit(solution)/shard_map/all_gather | solution.py:29
  26.2 1.8 convolution_bitcast_fusion.4
  27.9 284.2 %all-reduce.4 = bf16[256,512]{0,1:T(8,128)(2,1)S(1)} all-reduce(f32[256,512]{0,1:T(8,128)} %convolution_bitcast_fusion.4), channel_id=1, replica_groups=mesh['rows'=64,'cols'=8] {'rows'}, use_global_device_ids=true, to_apply=%region_1.0 | all-reduce | flops 131072 | bytes 786432 | tf_op jit(solution)/shard_map/psum | solution.py:31
  312.1 0.9 dynamic_update_slice.13
  313.0 0.9 fusion.7
  314.0 0.0 copy-start.2
  314.0 13.9 %all-gather.1 = bf16[256,512]{1,0:T(8,128)(2,1)} all-gather(bf16[32,512]{1,0:T(8,128)(2,1)S(1)} %fusion.7), channel_id=3, replica_groups=mesh['rows'=64,'cols'=8] {'cols'}, dimensions={0}, use_global_device_ids=true | all-gather | bytes 294912 | tf_op jit(solution)/shard_map/all_gather | solution.py:29
  327.9 1.0 reduce_sum.49
  328.9 1.8 convolution_bitcast_fusion.3
  330.7 280.2 %all-reduce.5 = bf16[256,512]{0,1:T(8,128)(2,1)} all-reduce(f32[256,512]{0,1:T(8,128)} %convolution_bitcast_fusion.3), channel_id=1, replica_groups=mesh['rows'=64,'cols'=8] {'rows'}, use_global_device_ids=true, to_apply=%region_3.0 | all-reduce | flops 131072 | bytes 786432 | tf_op jit(solution)/shard_map/psum | solution.py:31
  610.9 0.0 copy-done.2
  610.9 0.6 copy.13
  611.5 0.9 dynamic_update_slice.14
  612.4 1.2 fusion.9
  613.6 13.9 %all-gather.2 = bf16[256,512]{1,0:T(8,128)(2,1)} all-gather(bf16[32,512]{1,0:T(8,128)(2,1)S(1)} %fusion.9), channel_id=4, replica_groups=mesh['rows'=64,'cols'=8] {'cols'}, dimensions={0}, use_global_device_ids=true | all-gather | bytes 294912 | tf_op jit(solution)/shard_map/all_gather | solution.py:29
  627.6 1.0 reduce_sum.50
  628.6 1.8 convolution_bitcast_fusion.2
  630.3 278.0 %all-reduce.6 = bf16[256,512]{0,1:T(8,128)(2,1)} all-reduce(f32[256,512]{0,1:T(8,128)} %convolution_bitcast_fusion.2), channel_id=1, replica_groups=mesh['rows'=64,'cols'=8] {'rows'}, use_global_device_ids=true, to_apply=%region_5.0 | all-reduce | flops 131072 | bytes 786432 | tf_op jit(solution)/shard_map/psum | solution.py:31
  908.3 0.3 dynamic_update_slice.15
  908.7 1.4 fusion.8
  910.0 13.9 %all-gather.3 = bf16[256,512]{1,0:T(8,128)(2,1)} all-gather(bf16[32,512]{1,0:T(8,128)(2,1)S(1)} %fusion.8), channel_id=5, replica_groups=mesh['rows'=64,'cols'=8] {'cols'}, dimensions={0}, use_global_device_ids=true | all-gather | bytes 294912 | tf_op jit(solution)/shard_map/all_gather | solution.py:29
  924.0 1.0 reduce_sum.51
  924.9 1.8 convolution_bitcast_fusion.1
  926.7 280.0 %all-reduce.7 = bf16[256,512]{0,1:T(8,128)(2,1)} all-reduce(f32[256,512]{0,1:T(8,128)} %convolution_bitcast_fusion.1), channel_id=1, replica_groups=mesh['rows'=64,'cols'=8] {'rows'}, use_global_device_ids=true, to_apply=%region_7.0 | all-reduce | flops 131072 | bytes 786432 | tf_op jit(solution)/shard_map/psum | solution.py:31
  1206.7 0.0 copy-done
  1206.7 4.1 fusion.1
  1210.8 0.0 reduce-scatter.2.cloned.1.call-update
  1210.8 2.2 pad_maximum_fusion
  1213.0 0.0 copy-start.1
  1213.0 2.3 copy.11
  1215.3 31.3 %reduce-scatter.2.cloned.1.call-done = bf16[64,1536]{1,0:T(8,128)(2,1)} async-done(((bf16[512,1536]{1,0:T(8,128)(2,1)}), bf16[64,1536]{1,0:T(8,128)(2,1)}) %reduce-scatter.2.cloned.1.call-update) | async-done | bytes 196624 | tf_op jit(solution)/shard_map/reduce_scatter | solution.py:36
  1246.6 0.0 copy-done.1
  1246.6 1.6 subtract_convert_fusion
  (7 shorter events, 0.1 us)
Async XLA Ops:
  7.2 1199.6 %copy-start = (bf16[1536,4,256]{2,1,0:T(4,128)(2,1)S(1)}, bf16[1536,4,256]{2,1,0:T(4,128)(2,1)}, u32[]{:S(2)}) copy-start(bf16[1536,4,256]{2,1,0:T(4,128)(2,1)} %param.6) | copy-start | bytes 9437188
  7.2 1239.5 %reduce-scatter.2.cloned.1.call-start = ((), (), s32[]{:S(2)}) async-start(), calls=%async_computation.1 | async-start | bytes 1769472 | tf_op jit(solution)/shard_map/reduce_scatter | solution.py:36
  314.0 296.9 %copy-start.2 = (bf16[1,32,2,256]{3,2,1,0:T(2,128)(2,1)S(1)}, bf16[1,32,2,256]{3,2,1,0:T(2,128)(2,1)}, u32[]{:S(2)}) copy-start(bf16[1,32,2,256]{3,2,1,0:T(2,128)(2,1)} %slice.39) | copy-start | bytes 98308
  1213.0 33.6 %copy-start.1 = (bf16[64,1536]{1,0:T(8,128)(2,1)S(1)}, bf16[64,1536]{1,0:T(8,128)(2,1)}, u32[]{:S(2)}) copy-start(bf16[64,1536]{1,0:T(8,128)(2,1)} %param.9) | copy-start | bytes 589828
Sparse Core Ops, SparseCore 0:
  1211.0 35.6 reduce-scatter.1
